TPU v7x, 32 devices: a whole 2x2x4 slice. The times are simulated.
32 devices in a mesh: sample: 2 (over y), region: 4 (over x, core), sub: 4 (over z).
Axes of the slice: x: 2, y: 2, z: 4, core: 2. Of those that a mesh axis runs over, the one named last changes fastest.
Arguments:
- densities: bfloat16 [4096, 128], P(('sample', 'region', 'sub')), parts along dimension 0, may hold values from -6 to 6
- cluster_size: int32 [32], P('sample'), parts along dimension 0, may hold values from 1 to 128, 1365 in all
- near_block: bfloat16 [4096, 512], P(('sample', 'region', 'sub')), parts along dimension 0, may hold values from -0.25 to 0.25
- row_factor: bfloat16 [4096, 512], P(('sample', 'region', 'sub')), parts along dimension 0, may hold values from -0.375 to 0.375
- column_factor: bfloat16 [512, 4096], P(None, ('sample', 'region', 'sub')), parts along dimension 1, may hold values from -0.5 to 0.5
Outputs:
- applied: float32 [4096, 128], P(('sample', 'region', 'sub')), parts along dimension 0
There are 2 independent parts, one for each index of `sample`. A program takes and returns all parts, laid end to end along the dimension named above; each array names one. Nothing has to cross between parts.
Inputs may be any that keep to these rules, and one draw needn't show every extreme that they name: `cluster_size`: sizes of the 16 clusters, summing to 1365, with some cluster of exactly 128.
All inputs are finite; a program needn't handle non-finite values.
Results may differ from a plain program's by a relative error of at most 0.0022.
Values may be sent and summed in bfloat16 or wider, within the bound.
No kernel may reach another device: no remote copies, remote signals or barrier semaphores. Data moves between devices by JAX's collectives and lax.ppermute only.
A program may use at most 64 MiB of HBM per device.

v0:
```python
import jax
import jax.numpy as jnp
from jax import lax
from jax.sharding import PartitionSpec as P


def send_coefficients(coefficients):
    return lax.all_to_all(coefficients, ("region", "sub"), split_axis=0, concat_axis=0, tiled=True)


def local(densities, cluster_size, near_block, row_factor, column_factor):
    row_count, load_count = densities.shape
    group_count = lax.axis_size("sub")
    region_count = lax.axis_size("region")
    cluster_count = group_count * region_count
    rank_width = row_factor.shape[1] // cluster_count
    region_id = lax.axis_index("region")
    own_cluster = region_id * group_count + lax.axis_index("sub")
    slot_index = lax.broadcasted_iota(jnp.int32, (row_count, 1), 0)
    own_live = slot_index < cluster_size[own_cluster]
    masked = jnp.where(own_live, densities, jnp.zeros_like(densities))
    near_sum = jnp.dot(
        near_block,
        lax.all_gather(masked, "sub", axis=0, tiled=True),
        preferred_element_type=jnp.float32,
    )
    cluster_ids = jnp.arange(cluster_count, dtype=jnp.int32)
    far_flags = cluster_ids // group_count != region_id
    coefficients = jnp.dot(column_factor, masked, preferred_element_type=jnp.float32).astype(
        jnp.bfloat16
    )
    received = send_coefficients(coefficients)
    rank_flags = jnp.repeat(far_flags, rank_width)[:, None]
    received = jnp.where(rank_flags, received, jnp.zeros_like(received))
    far_sum = jnp.dot(row_factor, received, preferred_element_type=jnp.float32)
    combined = near_sum + far_sum
    return jnp.where(own_live, combined, jnp.zeros_like(combined))


def solution(mesh):
    return jax.shard_map(
        local,
        mesh=mesh,
        in_specs=(
            P(("sample", "region", "sub"), None),
            P("sample"),
            P(("sample", "region", "sub"), None),
            P(("sample", "region", "sub"), None),
            P(None, ("sample", "region", "sub")),
        ),
        out_specs=P(("sample", "region", "sub"), None),
        check_vma=False,
    )
```

profile of v0, /device:TPU:0, one launch (start us, length us, event | category | flops | bytes accessed | tf_op | source)
XLA Modules:
  0.0 28.1 jit_solution(1108674390602110613)
XLA Ops:
  0.0 0.0 copy-start
  0.0 0.0 copy-start.3
  0.0 0.7 %copy-done.3 = s32[16]{0:T(128)S(1)} copy-done((s32[16]{0:T(128)S(1)}, s32[16]{0:T(128)}, u32[]{:S(2)}) %copy-start.3) | copy-done | bytes 88
  0.7 0.6 %dynamic_slice.3 = s32[1]{0:T(128)} dynamic-slice(s32[16]{0:T(128)S(1)} %copy-done.3, s32[]{:T(128)S(6)} %select_n.23), dynamic_slice_sizes={1} | dynamic-slice | bytes 12 | tf_op jit(solution)/shard_map/dynamic_slice | solution.py:20
  1.3 0.6 %iota_compare_fusion = pred[128]{0:T(512)(128)(4,1)S(1)} fusion(s32[]{:T(128)} %bitcast), kind=kLoop, calls=%fused_computation.12 | loop fusion | flops 128 | bytes 132 | tf_op jit(solution)/shard_map/lt | solution.py:20
  1.9 0.8 %broadcast_select_fusion = bf16[128,128]{1,0:T(8,128)(2,1)S(1)} fusion(bf16[128,128]{1,0:T(8,128)(2,1)} %param.5, pred[128]{0:T(512)(128)(4,1)S(1)} %iota_compare_fusion), kind=kLoop, calls=%fused_computation.6 | loop fusion | flops 16384 | bytes 65664 | tf_op jit(solution)/shard_map/jit(_where)/select_n | solution.py:21
  2.8 0.0 copy-done
  2.8 0.2 fusion
  3.0 0.7 %copy.7 = bf16[512,128]{1,0:T(8,128)(2,1)} copy(bf16[512,128]{0,1:T(8,128)(2,1)S(1)} %fusion) | data formatting | bytes 262144 | tf_op jit(solution)/shard_map/convert_element_type | solution.py:29
  3.8 7.4 %all-to-all-start = ((bf16[16,32,128]{2,1,0:T(8,128)(2,1)}), bf16[16,32,128]{2,1,0:T(8,128)(2,1)S(1)}, u32[]{:S(2)}, u32[]{:S(2)}) async-start(bf16[16,32,128]{2,1,0:T(8,128)(2,1)} %bitcast.2), calls=%async_computation | async-start | bytes 262144 | tf_op jit(solution)/shard_map/all_to_all | solution.py:8
  11.2 0.0 copy-start.1
  11.2 14.7 %all_gather.3 = bf16[512,128]{1,0:T(8,128)(2,1)S(1)} all-gather(bf16[128,128]{1,0:T(8,128)(2,1)S(1)} %broadcast_select_fusion), channel_id=1, replica_groups=mesh['sample'=2,'region'=4,'sub'=4] {'sub'}, dimensions={0}, use_global_device_ids=true | all-gather | bytes 163840 | tf_op jit(solution)/shard_map/all_gather | solution.py:24
  25.8 0.1 broadcast_in_dim.41
  25.9 0.1 broadcast_in_dim.42
  26.0 0.0 copy-done.1
  26.0 0.2 fusion.4
  26.2 0.0 copy-start.2
  26.2 0.0 all-to-all-done
  26.3 0.1 bitcast_select_fusion
  26.4 0.7 %copy-done.2 = bf16[128,512]{1,0:T(8,128)(2,1)S(1)} copy-done((bf16[128,512]{1,0:T(8,128)(2,1)S(1)}, bf16[128,512]{1,0:T(8,128)(2,1)}, u32[]{:S(2)}) %copy-start.2) | copy-done | bytes 131096
  27.1 0.2 fusion.2
  27.4 0.7 %copy.8 = f32[128,128]{1,0:T(8,128)} copy(f32[128,128]{0,1:T(8,128)S(1)} %fusion.2) | data formatting | bytes 131072 | tf_op jit(solution)/shard_map/jit(_where)/select_n | solution.py:37
  (1 shorter events, 0.0 us)
Async XLA Ops:
  0.0 2.8 %copy-start = (bf16[512,128]{1,0:T(8,128)(2,1)S(1)}, bf16[512,128]{1,0:T(8,128)(2,1)}, u32[]{:S(2)}) copy-start(bf16[512,128]{1,0:T(8,128)(2,1)} %param.9) | copy-start | bytes 393220
  0.0 0.7 %copy-start.3 = (s32[16]{0:T(128)S(1)}, s32[16]{0:T(128)}, u32[]{:S(2)}) copy-start(s32[16]{0:T(128)} %param.6) | copy-start | bytes 196
  3.8 22.5 %all-to-all-start = ((bf16[16,32,128]{2,1,0:T(8,128)(2,1)}), bf16[16,32,128]{2,1,0:T(8,128)(2,1)S(1)}, u32[]{:S(2)}, u32[]{:S(2)}) async-start(bf16[16,32,128]{2,1,0:T(8,128)(2,1)} %bitcast.2), calls=%async_computation | async-start | bytes 262144 | tf_op jit(solution)/shard_map/all_to_all | solution.py:8
  11.2 14.9 %copy-start.1 = (bf16[128,512]{1,0:T(8,128)(2,1)S(1)}, bf16[128,512]{1,0:T(8,128)(2,1)}, u32[]{:S(2)}) copy-start(bf16[128,512]{1,0:T(8,128)(2,1)} %param.7) | copy-start | bytes 393220
  26.2 0.9 %copy-start.2 = (bf16[128,512]{1,0:T(8,128)(2,1)S(1)}, bf16[128,512]{1,0:T(8,128)(2,1)}, u32[]{:S(2)}) copy-start(bf16[128,512]{1,0:T(8,128)(2,1)} %param.8) | copy-start | bytes 393220
where the time goes:
time: 28.4 us; the launch traced here: 28.1 us
  blocking collectives  14.7 us (52%)
  starting transfers between devices  7.39 us (26%)
  local copies, waits for them, and re-layouts  3.67 us (13%)
  other arithmetic  1.64 us (6%)
  matrix products  0.65 us (2%)
    all_gather x1, blocking collectives, local(): lax.all_gather(masked, 'sub', axis=0, tiled=True)  14.7 us
    all_to_all x1, starting transfers between devices, send_coefficients(): lax.all_to_all(coefficients, ('region', 'sub'), split_axis=0, concat_axis...  7.39 us
    unnamed x8, local copies, waits for them, and re-layouts  1.45 us
    select_n x1, other arithmetic, local(): masked = jnp.where(own_live, densities, jnp.zeros_like(densities))  0.84 us
    convert_element_type x1, local copies, waits for them, and re-layouts, local(): jnp.dot(column_factor, masked, preferred_element_type=jnp.float32)  0.75 us
    select_n x1, local copies, waits for them, and re-layouts, local(): return jnp.where(own_live, combined, jnp.zeros_like(combined))  0.73 us
    lt x1, other arithmetic, local(): own_live = slot_index < cluster_size[own_cluster]  0.65 us
    dynamic_slice x1, local copies, waits for them, and re-layouts, local(): own_live = slot_index < cluster_size[own_cluster]  0.58 us
  transfers between devices with their start and end apart: 1, of which 0 were waited for; matrix products, arithmetic and copies ran while one was open for 1% of the time, Pallas kernels for 0%

commit v1 on v0

--- a/solution.py
+++ b/solution.py
@@ -2,6 +2,32 @@
 import jax.numpy as jnp
 from jax import lax
 from jax.sharding import PartitionSpec as P
+from jax.lax import axis_index, axis_size, ppermute
+
+
+def edit_the_sums_all(x_local):
+    f_next = axis_index("sub")
+    t_next = axis_size("sub")
+    arr_out, carry_in, ready = (t_next, f_next, x_local.shape[0])
+    slots = [dev * arr_out if idx == 0 else dev for idx, dev in enumerate(x_local.shape)]
+    outcome_arr = jnp.zeros(slots, x_local.dtype)
+    arr_next = spare = x_local
+    step_out = lax.dynamic_update_slice_in_dim(outcome_arr, x_local, carry_in * ready, axis=0)
+    for k0 in tuple(range(1, arr_out // 2 + 1)):
+        arr_next = ppermute(
+            arr_next, axis_name="sub", perm=[(idx, (idx + 1) % arr_out) for idx in range(arr_out)]
+        )
+        step_out = lax.dynamic_update_slice_in_dim(
+            step_out, arr_next, (carry_in - k0) % arr_out * ready, axis=0
+        )
+        if 2 * k0 < arr_out:
+            spare = ppermute(
+                spare, axis_name="sub", perm=[(idx, (idx - 1) % arr_out) for idx in range(arr_out)]
+            )
+            step_out = lax.dynamic_update_slice_in_dim(
+                step_out, spare, (carry_in + k0) % arr_out * ready, axis=0
+            )
+    return step_out
 
 
 def send_coefficients(coefficients):
@@ -19,11 +45,7 @@
     slot_index = lax.broadcasted_iota(jnp.int32, (row_count, 1), 0)
     own_live = slot_index < cluster_size[own_cluster]
     masked = jnp.where(own_live, densities, jnp.zeros_like(densities))
-    near_sum = jnp.dot(
-        near_block,
-        lax.all_gather(masked, "sub", axis=0, tiled=True),
-        preferred_element_type=jnp.float32,
-    )
+    near_sum = jnp.dot(near_block, edit_the_sums_all(masked), preferred_element_type=jnp.float32)
     cluster_ids = jnp.arange(cluster_count, dtype=jnp.int32)
     far_flags = cluster_ids // group_count != region_id
     coefficients = jnp.dot(column_factor, masked, preferred_element_type=jnp.float32).astype(

time: 28.4 us -> 25.8 us (0.908)
  blocking collectives: 14.7 us -> 0 us
  starting transfers between devices: 7.39 us -> 13.2 us
  waiting for transfers between devices: 0.01 us -> 5.51 us
  local copies, waits for them, and re-layouts: 3.67 us -> 5.13 us
  other arithmetic: 1.64 us -> 0.89 us
    all_gather x1 -> x0, blocking collectives: 14.7 us -> none  [local(): lax.all_gather(masked, 'sub', axis=0, tiled=True)]
    ppermute x0 -> x3, starting transfers between devices: none -> 7.06 us  [the longest x1 5.13 us: edit_the_sums_all(): ppermute(spare, axis_name='sub', perm=[(idx, (idx - 1) % arr_out) for idx...]
    ppermute x0 -> x3, waiting for transfers between devices: none -> 5.51 us  [the longest x2 5.5 us: edit_the_sums_all(): ppermute(arr_next, axis_name='sub', perm=[(idx, (idx + 1) % arr_out) for...]
    unnamed x8 -> x10, local copies, waits for them, and re-layouts: 1.45 us -> 2.85 us
    all_to_all x1, starting transfers between devices: 7.39 us -> 6.13 us  [send_coefficients(): lax.all_to_all(coefficients, ('region', 'sub'), split_axis=0, concat_axis...]
    select_n x1 -> x0, other arithmetic: 0.84 us -> none  [local(): masked = jnp.where(own_live, densities, jnp.zeros_like(densities))]
  transfers between devices with their start and end apart: 1 -> 4, of which waited for: 0 -> 1; matrix products, arithmetic and copies ran while one was open for 1% -> 5% of each run, Pallas kernels for 0% -> 0%
where the time goes in v1:
time: 25.8 us; the launch traced here: 25.5 us
  starting transfers between devices  13.2 us (51%)
  waiting for transfers between devices  5.51 us (21%)
  local copies, waits for them, and re-layouts  5.13 us (20%)
  other arithmetic  0.89 us (3%)
  matrix products  0.65 us (3%)
    all_to_all x1, starting transfers between devices, send_coefficients(): lax.all_to_all(coefficients, ('region', 'sub'), split_axis=0, concat_axis...  6.13 us
    ppermute x2, waiting for transfers between devices, edit_the_sums_all(): ppermute(arr_next, axis_name='sub', perm=[(idx, (idx + 1) % arr_out) for...  5.5 us
    ppermute x1, starting transfers between devices, edit_the_sums_all(): ppermute(spare, axis_name='sub', perm=[(idx, (idx - 1) % arr_out) for idx...  5.13 us
    unnamed x10, local copies, waits for them, and re-layouts  2.85 us
    ppermute x2, starting transfers between devices, edit_the_sums_all(): ppermute(arr_next, axis_name='sub', perm=[(idx, (idx + 1) % arr_out) for...  1.93 us
    convert_element_type x1, local copies, waits for them, and re-layouts, local(): jnp.dot(column_factor, masked, preferred_element_type=jnp.float32)  0.75 us
    select_n x1, local copies, waits for them, and re-layouts, local(): return jnp.where(own_live, combined, jnp.zeros_like(combined))  0.73 us
    lt x1, other arithmetic, local(): own_live = slot_index < cluster_size[own_cluster]  0.65 us
  transfers between devices with their start and end apart: 4, of which 1 were waited for; matrix products, arithmetic and copies ran while one was open for 5% of the time, Pallas kernels for 0%

profile of v1, /device:TPU:0, one launch (start us, length us, event | category | flops | bytes accessed | tf_op | source)
XLA Modules:
  0.0 25.5 jit_solution(13145799297912497453)
XLA Ops:
  0.0 0.0 copy-start
  0.0 0.0 copy-start.4
  0.0 0.7 %copy-done.4 = s32[16]{0:T(128)S(1)} copy-done((s32[16]{0:T(128)S(1)}, s32[16]{0:T(128)}, u32[]{:S(2)}) %copy-start.4) | copy-done | bytes 88
  0.7 0.6 %dynamic_slice.3 = s32[1]{0:T(128)} dynamic-slice(s32[16]{0:T(128)S(1)} %copy-done.4, s32[]{:T(128)S(6)} %select_n.50), dynamic_slice_sizes={1} | dynamic-slice | bytes 12 | tf_op jit(solution)/shard_map/dynamic_slice | solution.py:46
  1.3 0.6 %iota_compare_fusion = pred[128]{0:T(512)(128)(4,1)S(1)} fusion(s32[]{:T(128)} %bitcast), kind=kLoop, calls=%fused_computation.16 | loop fusion | flops 128 | bytes 132 | tf_op jit(solution)/shard_map/lt | solution.py:46
  1.9 0.0 copy-start.3
  2.0 0.7 %copy-done.3 = bf16[128,128]{1,0:T(8,128)(2,1)S(1)} copy-done((bf16[128,128]{1,0:T(8,128)(2,1)S(1)}, bf16[128,128]{1,0:T(8,128)(2,1)}, u32[]{:S(2)}) %copy-start.3) | copy-done | bytes 32792
  2.7 0.1 constant_dynamic-update-slice_fusion.3
  2.8 5.1 %collective-permute-start.1 = (bf16[128,128]{1,0:T(8,128)(2,1)S(1)}, bf16[128,128]{1,0:T(8,128)(2,1)S(1)}, u32[]{:S(2)}, u32[]{:S(2)}) collective-permute-start(bf16[128,128]{1,0:T(8,128)(2,1)S(1)} %get-tuple-element.6), channel_id=1, source_target_pairs={{0,3},{1,0},{2,1},{3,2},{4,7},{5,4},{6,5},{7,6},{8,11},{9,8},{10,9... | collective-permute-start | bytes 98312 | tf_op jit(solution)/shard_map/ppermute | solution.py:24
  7.9 0.0 collective-permute-start
  7.9 0.0 copy-done
  7.9 0.2 fusion
  8.1 0.7 %copy.8 = bf16[512,128]{1,0:T(8,128)(2,1)} copy(bf16[512,128]{0,1:T(8,128)(2,1)S(1)} %fusion) | data formatting | bytes 262144 | tf_op jit(solution)/shard_map/convert_element_type | solution.py:51
  8.9 6.1 %all-to-all-start = ((bf16[16,32,128]{2,1,0:T(8,128)(2,1)}), bf16[16,32,128]{2,1,0:T(8,128)(2,1)S(1)}, u32[]{:S(2)}, u32[]{:S(2)}) async-start(bf16[16,32,128]{2,1,0:T(8,128)(2,1)} %bitcast.2), calls=%async_computation | async-start | bytes 262144 | tf_op jit(solution)/shard_map/all_to_all | solution.py:34
  15.1 0.1 broadcast_in_dim.38
  15.2 0.1 broadcast_in_dim.39
  15.3 0.0 collective-permute-done
  15.3 1.9 %collective-permute-start.2 = (bf16[128,128]{1,0:T(8,128)(2,1)S(1)}, bf16[128,128]{1,0:T(8,128)(2,1)S(1)}, u32[]{:S(2)}, u32[]{:S(2)}) collective-permute-start(bf16[128,128]{1,0:T(8,128)(2,1)S(1)} %collective-permute-done), channel_id=1, source_target_pairs={{0,1},{1,2},{2,3},{3,0},{4,5},{5,6},{6,7},{7,4},{8,9},{9,10},{10,1... | collective-permute-start | bytes 98312 | tf_op jit(solution)/shard_map/ppermute | solution.py:17
  17.2 0.0 collective-permute-done.1
  17.2 5.5 %collective-permute-done.2 = bf16[128,128]{1,0:T(8,128)(2,1)S(1)} collective-permute-done((bf16[128,128]{1,0:T(8,128)(2,1)S(1)}, bf16[128,128]{1,0:T(8,128)(2,1)S(1)}, u32[]{:S(2)}, u32[]{:S(2)}) %collective-permute-start.2) | collective-permute-done | bytes 32800 | tf_op jit(solution)/shard_map/ppermute | solution.py:17
  22.7 0.0 copy-start.1
  22.7 0.0 all-to-all-done
  22.8 0.1 bitcast_select_fusion
  22.9 0.7 %copy-done.1 = bf16[128,512]{1,0:T(8,128)(2,1)S(1)} copy-done((bf16[128,512]{1,0:T(8,128)(2,1)S(1)}, bf16[128,512]{1,0:T(8,128)(2,1)}, u32[]{:S(2)}) %copy-start.1) | copy-done | bytes 131096
  23.6 0.0 copy-start.2
  23.6 0.2 fusion.4
  23.9 0.7 %copy-done.2 = bf16[128,512]{1,0:T(8,128)(2,1)S(1)} copy-done((bf16[128,512]{1,0:T(8,128)(2,1)S(1)}, bf16[128,512]{1,0:T(8,128)(2,1)}, u32[]{:S(2)}) %copy-start.2) | copy-done | bytes 131096
  24.5 0.2 fusion.2
  24.8 0.7 %copy.9 = f32[128,128]{1,0:T(8,128)} copy(f32[128,128]{0,1:T(8,128)S(1)} %fusion.2) | data formatting | bytes 131072 | tf_op jit(solution)/shard_map/jit(_where)/select_n | solution.py:59
  (5 shorter events, 0.1 us)
Async XLA Ops:
  0.0 7.9 %copy-start = (bf16[512,128]{1,0:T(8,128)(2,1)S(1)}, bf16[512,128]{1,0:T(8,128)(2,1)}, u32[]{:S(2)}) copy-start(bf16[512,128]{1,0:T(8,128)(2,1)} %param.9) | copy-start | bytes 393220
  0.0 0.7 %copy-start.4 = (s32[16]{0:T(128)S(1)}, s32[16]{0:T(128)}, u32[]{:S(2)}) copy-start(s32[16]{0:T(128)} %param.6) | copy-start | bytes 196
  1.9 0.8 %copy-start.3 = (bf16[128,128]{1,0:T(8,128)(2,1)S(1)}, bf16[128,128]{1,0:T(8,128)(2,1)}, u32[]{:S(2)}) copy-start(bf16[128,128]{1,0:T(8,128)(2,1)} %param.5) | copy-start | bytes 98308
  2.8 14.4 %collective-permute-start.1 = (bf16[128,128]{1,0:T(8,128)(2,1)S(1)}, bf16[128,128]{1,0:T(8,128)(2,1)S(1)}, u32[]{:S(2)}, u32[]{:S(2)}) collective-permute-start(bf16[128,128]{1,0:T(8,128)(2,1)S(1)} %get-tuple-element.6), channel_id=1, source_target_pairs={{0,3},{1,0},{2,1},{3,2},{4,7},{5,4},{6,5},{7,6},{8,11},{9,8},{10,9... | collective-permute-start | bytes 98312 | tf_op jit(solution)/shard_map/ppermute | solution.py:24
  7.9 7.3 %collective-permute-start = (bf16[128,128]{1,0:T(8,128)(2,1)S(1)}, bf16[128,128]{1,0:T(8,128)(2,1)S(1)}, u32[]{:S(2)}, u32[]{:S(2)}) collective-permute-start(bf16[128,128]{1,0:T(8,128)(2,1)S(1)} %get-tuple-element.6), channel_id=1, source_target_pairs={{0,1},{1,2},{2,3},{3,0},{4,5},{5,6},{6,7},{7,4},{8,9},{9,10},{10,1... | collective-permute-start | bytes 98312 | tf_op jit(solution)/shard_map/ppermute | solution.py:17
  8.9 13.9 %all-to-all-start = ((bf16[16,32,128]{2,1,0:T(8,128)(2,1)}), bf16[16,32,128]{2,1,0:T(8,128)(2,1)S(1)}, u32[]{:S(2)}, u32[]{:S(2)}) async-start(bf16[16,32,128]{2,1,0:T(8,128)(2,1)} %bitcast.2), calls=%async_computation | async-start | bytes 262144 | tf_op jit(solution)/shard_map/all_to_all | solution.py:34
  15.3 7.5 %collective-permute-start.2 = (bf16[128,128]{1,0:T(8,128)(2,1)S(1)}, bf16[128,128]{1,0:T(8,128)(2,1)S(1)}, u32[]{:S(2)}, u32[]{:S(2)}) collective-permute-start(bf16[128,128]{1,0:T(8,128)(2,1)S(1)} %collective-permute-done), channel_id=1, source_target_pairs={{0,1},{1,2},{2,3},{3,0},{4,5},{5,6},{6,7},{7,4},{8,9},{9,10},{10,1... | collective-permute-start | bytes 98312 | tf_op jit(solution)/shard_map/ppermute | solution.py:17
  22.7 0.9 %copy-start.1 = (bf16[128,512]{1,0:T(8,128)(2,1)S(1)}, bf16[128,512]{1,0:T(8,128)(2,1)}, u32[]{:S(2)}) copy-start(bf16[128,512]{1,0:T(8,128)(2,1)} %param.8) | copy-start | bytes 393220
  23.6 0.9 %copy-start.2 = (bf16[128,512]{1,0:T(8,128)(2,1)S(1)}, bf16[128,512]{1,0:T(8,128)(2,1)}, u32[]{:S(2)}) copy-start(bf16[128,512]{1,0:T(8,128)(2,1)} %param.7) | copy-start | bytes 393220
